TPU v7x, 256 devices: a whole 4x4x8 slice. The times are simulated.
256 devices in a mesh: vocab: 64 (over y, z, core), hidden: 4 (over x).
Axes of the slice: x: 4, y: 4, z: 8, core: 2. Of those that a mesh axis runs over, the one named last changes fastest.
Arguments:
- states: bfloat16 [1024, 7168], P(('vocab', 'hidden')), may hold values from -32 to 32
- head: bfloat16 [7168, 129280], P('hidden', 'vocab'), may hold values from -1 to 1
Outputs:
- logp: float32 [1024, 129280], P('hidden', 'vocab')
All inputs are finite; a program needn't handle non-finite values.
Results may differ from a plain program's by a relative error of at most 0.0003.
Values may be sent and summed in bfloat16 or wider, within the bound.
A program may use at most 128 MiB of HBM per device.

v0:
```python
import math
import jax
import jax.numpy as jnp
from jax import lax
from jax.sharding import Mesh
from jax.sharding import PartitionSpec as P

VOCAB = ("vocab_0", "vocab_1", "vocab_2")
VOCAB_HIDDEN = ("vocab_0", "vocab_1", "vocab_2", "hidden")
sharpness = 4.0
minp_offset = math.log(10.0)
logp_floor = 30.0


def joined_along(pieces, dim):
    pieces = jnp.moveaxis(pieces, 0, dim)
    dims = pieces.shape
    return pieces.reshape(*dims[:dim], dims[dim] * dims[dim + 1], *dims[dim + 2 :])


def gather_in_order(shard, axes, order):
    pieces = shard
    for k in order:
        pieces = lax.all_gather(pieces, axes[k])
    done = order[::-1]
    back = [done.index(k) for k in range(len(axes))]
    pieces = pieces.transpose(*back, *range(len(axes), pieces.ndim))
    return pieces.reshape(-1, *shard.shape)


def gather_axes(shard, axes, order, dim):
    return joined_along(gather_in_order(shard, axes, order), dim)


def from_everyone(shard, axis):
    devices = lax.axis_size(axis)
    return lax.all_to_all(
        jnp.broadcast_to(shard[None], (devices, *shard.shape)), axis, 0, 0, tiled=True
    )


def over_copies(shard, axis):
    return from_everyone(shard, axis).max(axis=0)


def over_copies_2(shard, axis):
    return from_everyone(shard, axis).sum(axis=0)


def filtered(logits, top):
    shifted = logits - top[:, None]
    return shifted + jax.nn.log_sigmoid(sharpness * (shifted + minp_offset))


def body(states, head):
    slices = lax.all_to_all(states, "hidden", split_axis=1, concat_axis=0, tiled=True)
    gathered = gather_axes(slices, VOCAB, (0, 1, 2), 0)
    logits = lax.psum_scatter(
        jnp.dot(gathered, head, preferred_element_type=jnp.float32),
        "hidden",
        scatter_dimension=0,
        tiled=True,
    )
    top = over_copies(jnp.max(logits, axis=1), VOCAB)
    gated = filtered(logits, top)
    total = over_copies_2(jnp.sum(jnp.exp(gated), axis=1), VOCAB)
    return jnp.maximum(gated - jnp.log(total)[:, None], -logp_floor)


def solution(mesh):
    torus = Mesh(
        mesh.devices.reshape(4, 8, 2, mesh.shape["hidden"]),
        ("vocab_0", "vocab_1", "vocab_2", "hidden"),
    )
    return jax.shard_map(
        body,
        mesh=torus,
        in_specs=(P(VOCAB_HIDDEN, None), P("hidden", VOCAB)),
        out_specs=P("hidden", VOCAB),
        check_vma=False,
    )
```

profile of v0, /device:TPU:1, one launch (start us, length us, event | category | flops | bytes accessed | tf_op | source)
XLA Modules:
  0.0 236.1 jit_solution(12771082451407229781)
XLA Ops:
  6.5 0.0 all-gather.5.cloned.1.call-start
  6.5 9.3 %all_to_all.28 = bf16[4,4,1792]{2,0,1:T(4,128)(2,1)S(1)} all-to-all(bf16[4,4,1792]{2,0,1:T(4,128)(2,1)} %bitcast.13), channel_id=1, replica_groups=mesh['vocab_0'=4,'vocab_1'=8,'vocab_2'=2,'hidden'=4] {'hidden'}, dimensions={1} | all-to-all | bytes 114688 | tf_op jit(solution)/shard_map/all_to_all | solution.py:56
  15.8 10.6 %all_gather.19 = bf16[4,16,1792]{2,1,0:T(8,128)(2,1)} all-gather(bf16[1,16,1792]{2,1,0:T(8,128)(2,1)S(1)} %all_gather.18), channel_id=1, replica_groups=mesh['vocab_0'=4,'vocab_1'=8,'vocab_2'=2,'hidden'=4] {'vocab_0'}, dimensions={0}, use_global_device_ids=true | all-gather | bytes 286720 | tf_op jit(solution)/shard_map/all_gather | solution.py:24
  26.4 0.0 all-gather.5.cloned.1.call-update
  26.4 0.0 all-gather.7.cloned.1.call-start
  26.5 41.7 %all-gather.5.cloned.1.call-done = bf16[32,16,1792]{2,1,0:T(8,128)(2,1)} async-done(((bf16[4,16,1792]{2,1,0:T(8,128)(2,1)}), bf16[32,16,1792]{2,1,0:T(8,128)(2,1)}) %all-gather.5.cloned.1.call-update) | async-done | bytes 1835024 | tf_op jit(solution)/shard_map/all_gather | solution.py:24
  68.2 0.0 all-gather.7.cloned.1.call-update
  68.2 0.0 reduce-scatter.2.cloned.1.call-start
  68.3 23.0 %all-gather.7.cloned.1.call-done = bf16[16,4,16,1792]{3,2,1,0:T(8,128)(2,1)} async-done(((bf16[8,4,16,1792]{3,2,1,0:T(8,128)(2,1)}), bf16[16,4,16,1792]{3,2,1,0:T(8,128)(2,1)}) %all-gather.7.cloned.1.call-update) | async-done | bytes 3670032 | tf_op jit(solution)/shard_map/all_gather | solution.py:24
  91.3 0.0 copy-start.1
  91.3 2.6 %copy.11 = bf16[4,8,2,16,1792]{4,3,2,1,0:T(8,128)(2,1)S(1)} copy(bf16[4,8,2,16,1792]{4,3,0,1,2:T(8,128)(2,1)} %bitcast.9) | data formatting | bytes 7340032 | tf_op jit(solution)/shard_map/transpose | solution.py:27
  93.9 1.6 copy-done.1
  95.4 10.3 %fusion.2 = f32[1024,2020]{0,1:T(8,128)} fusion(bf16[1024,1792]{1,0:T(8,128)(2,1)S(1)} %bitcast.10, bf16[1792,2020]{0,1:T(8,128)(2,1)S(1)} %copy-done.1), kind=kOutput, calls=%fused_computation.5 | convolution fusion | flops 7413432320 | bytes 19183616 | tf_op jit(solution)/shard_map/dot_general | solution.py:59
  105.7 0.0 reduce-scatter.2.cloned.1.call-update
  105.7 83.2 %reduce-scatter.2.cloned.1.call-done = f32[256,2020]{0,1:T(8,128)} async-done(((f32[1024,2020]{0,1:T(8,128)}), f32[256,2020]{0,1:T(8,128)}) %reduce-scatter.2.cloned.1.call-update) | async-done | bytes 2068496 | tf_op jit(solution)/shard_map/reduce_scatter | solution.py:58
  188.9 0.0 copy-start
  188.9 2.0 reduce_max.18
  191.0 20.2 %all_to_all.29 = f32[64,1,256]{2,1,0:T(1,128)S(1)} all-to-all(f32[64,1,256]{2,1,0:T(1,128)S(1)} %broadcast_in_dim.4), channel_id=1, replica_groups=mesh['vocab_0'=4,'vocab_1'=8,'vocab_2'=2,'hidden'=4] {'vocab_0','vocab_1..., dimensions={0} | all-to-all | bytes 131072 | tf_op jit(solution)/shard_map/all_to_all | solution.py:37
  211.2 0.1 reduce_max.19
  211.3 0.0 copy-done
  211.3 1.6 exponential_reduce_fusion
  213.0 13.6 %all_to_all.30 = f32[64,1,256]{2,1,0:T(1,128)S(1)} all-to-all(f32[64,1,256]{2,1,0:T(1,128)S(1)} %broadcast_in_dim.5), channel_id=1, replica_groups=mesh['vocab_0'=4,'vocab_1'=8,'vocab_2'=2,'hidden'=4] {'vocab_0','vocab_1..., dimensions={0} | all-to-all | bytes 131072 | tf_op jit(solution)/shard_map/all_to_all | solution.py:37
  226.6 0.1 reduce_sum.19
  226.7 2.9 %subtract_maximum_fusion = f32[256,2020]{0,1:T(8,128)} fusion(f32[256]{0:T(256)S(1)} %log.7, f32[256,2020]{0,1:T(8,128)S(1)} %copy-done, f32[256]{0:T(256)S(1)} %reduce_max.19), kind=kLoop, calls=%fused_computation.3 | loop fusion | flops 7239680 | bytes 4139008 | tf_op jit(solution)/shard_map/max | solution.py:67
  (4 shorter events, 0.1 us)
Async XLA Ops:
  6.5 61.7 %all-gather.5.cloned.1.call-start = ((), (), s32[]{:S(2)}) async-start(), calls=%async_computation.5 | async-start | bytes 2064384 | tf_op jit(solution)/shard_map/all_gather | solution.py:24
  26.4 64.9 %all-gather.7.cloned.1.call-start = ((), (), s32[]{:S(2)}) async-start(), calls=%async_computation.6 | async-start | bytes 5505024 | tf_op jit(solution)/shard_map/all_gather | solution.py:24
  68.2 120.7 %reduce-scatter.2.cloned.1.call-start = ((), (), s32[]{:S(2)}) async-start(), calls=%async_computation.4 | async-start | bytes 10362880 | tf_op jit(solution)/shard_map/reduce_scatter | solution.py:58
  91.3 4.2 %copy-start.1 = (bf16[1792,2020]{0,1:T(8,128)(2,1)S(1)}, bf16[1792,2020]{0,1:T(8,128)(2,1)}, u32[]{:S(2)}) copy-start(bf16[1792,2020]{0,1:T(8,128)(2,1)} %param.3) | copy-start | bytes 21719044
  188.9 22.4 %copy-start = (f32[256,2020]{0,1:T(8,128)S(1)}, f32[256,2020]{0,1:T(8,128)}, u32[]{:S(2)}) copy-start(f32[256,2020]{0,1:T(8,128)} %reduce-scatter.2.cloned.1.call-done) | copy-start | bytes 6205444
Sparse Core Ops, SparseCore 0:
  26.5 41.6 all-gather.4
  70.0 21.2 all-gather.6
  105.9 82.9 reduce-scatter.1
where the time goes:
time: 236 us
  waiting for transfers between devices  148 us (63%)
  blocking collectives  53.7 us (23%)
  between operations  13.1 us (6%)
  matrix products  10.3 us (4%)
  other arithmetic  6.69 us (3%)
  local copies, waits for them, and re-layouts  4.26 us (2%)
    reduce_scatter x1, waiting for transfers between devices, body(): lax.psum_scatter(jnp.dot(gathered, head, preferred_element_type=jnp.float...  83.2 us
    all_gather x2, waiting for transfers between devices, gather_in_order(): pieces = lax.all_gather(pieces, axes[k])  64.7 us
    all_to_all x2, blocking collectives, from_everyone(): lax.all_to_all(jnp.broadcast_to(shard[None], (devices, *shard.shape)), ax...  33.9 us
    all_gather x1, blocking collectives, gather_in_order(): pieces = lax.all_gather(pieces, axes[k])  10.6 us
    dot_general x1, matrix products, body(): jnp.dot(gathered, head, preferred_element_type=jnp.float32)  10.3 us
    all_to_all x1, blocking collectives, body(): lax.all_to_all(states, 'hidden', split_axis=1, concat_axis=0, tiled=True)  9.27 us
  transfers between devices with their start and end apart: 3, of which 3 were waited for; matrix products, arithmetic and copies ran while one was open for 0% of the time, Pallas kernels for 0%

commit v1 on v0

--- a/solution.py
+++ b/solution.py
@@ -53,7 +53,12 @@
 
 
 def body(states, head):
-    slices = lax.all_to_all(states, "hidden", split_axis=1, concat_axis=0, tiled=True)
+    slices = jnp.concatenate(
+        lax.all_to_all(
+            jnp.stack(jnp.split(states, lax.axis_size("hidden"), axis=1)), "hidden", 0, 0
+        ),
+        axis=0,
+    )
     gathered = gather_axes(slices, VOCAB, (0, 1, 2), 0)
     logits = lax.psum_scatter(
         jnp.dot(gathered, head, preferred_element_type=jnp.float32),

time: 236 us -> 237 us (level)
  no operation moved by 1% of the time
where the time goes in v1:
time: 237 us
  waiting for transfers between devices  148 us (62%)
  blocking collectives  53.5 us (23%)
  between operations  13.1 us (6%)
  matrix products  10.3 us (4%)
  other arithmetic  6.74 us (3%)
  local copies, waits for them, and re-layouts  5.05 us (2%)
    reduce_scatter x1, waiting for transfers between devices, body(): lax.psum_scatter(jnp.dot(gathered, head, preferred_element_type=jnp.float...  83.2 us
    all_gather x2, waiting for transfers between devices, gather_in_order(): pieces = lax.all_gather(pieces, axes[k])  64.7 us
    all_to_all x2, blocking collectives, from_everyone(): lax.all_to_all(jnp.broadcast_to(shard[None], (devices, *shard.shape)), ax...  33.8 us
    all_gather x1, blocking collectives, gather_in_order(): pieces = lax.all_gather(pieces, axes[k])  10.6 us
    dot_general x1, matrix products, body(): jnp.dot(gathered, head, preferred_element_type=jnp.float32)  10.3 us
    all_to_all x1, blocking collectives, body(): lax.all_to_all(jnp.stack(jnp.split(states, lax.axis_size('hidden'), axis=...  9.08 us
  transfers between devices with their start and end apart: 3, of which 3 were waited for; matrix products, arithmetic and copies ran while one was open for 0% of the time, Pallas kernels for 0%

profile of v1, /device:TPU:1, one launch (start us, length us, event | category | flops | bytes accessed | tf_op | source)
XLA Modules:
  0.0 236.7 jit_solution(7088764140589157440)
XLA Ops:
  6.5 0.0 all-gather.5.cloned.1.call-start
  6.5 0.8 slice_bitcast_fusion.3
  7.3 0.1 pad_maximum_fusion
  7.4 9.1 %all_to_all.17 = bf16[4,4,1792]{2,1,0:T(4,128)(2,1)S(1)} all-to-all(bf16[4,4,1792]{2,1,0:T(4,128)(2,1)S(1)} %pad_maximum_fusion), channel_id=1, replica_groups=mesh['vocab_0'=4,'vocab_1'=8,'vocab_2'=2,'hidden'=4] {'hidden'}, dimensions={0} | all-to-all | bytes 114688 | tf_op jit(solution)/shard_map/all_to_all | solution.py:57
  16.5 10.6 %all_gather.15 = bf16[4,16,1792]{2,1,0:T(8,128)(2,1)} all-gather(bf16[1,16,1792]{2,1,0:T(8,128)(2,1)S(1)} %all_gather_reshape.3), channel_id=1, replica_groups=mesh['vocab_0'=4,'vocab_1'=8,'vocab_2'=2,'hidden'=4] {'vocab_0'}, dimensions={0}, use_global_device_ids=true | all-gather | bytes 286720 | tf_op jit(solution)/shard_map/all_gather | solution.py:24
  27.0 0.0 all-gather.5.cloned.1.call-update
  27.1 0.0 all-gather.7.cloned.1.call-start
  27.1 41.7 %all-gather.5.cloned.1.call-done = bf16[32,16,1792]{2,1,0:T(8,128)(2,1)} async-done(((bf16[4,16,1792]{2,1,0:T(8,128)(2,1)}), bf16[32,16,1792]{2,1,0:T(8,128)(2,1)}) %all-gather.5.cloned.1.call-update) | async-done | bytes 1835024 | tf_op jit(solution)/shard_map/all_gather | solution.py:24
  68.8 0.0 all-gather.7.cloned.1.call-update
  68.9 0.0 reduce-scatter.2.cloned.1.call-start
  68.9 23.0 %all-gather.7.cloned.1.call-done = bf16[16,4,16,1792]{3,2,1,0:T(8,128)(2,1)} async-done(((bf16[8,4,16,1792]{3,2,1,0:T(8,128)(2,1)}), bf16[16,4,16,1792]{3,2,1,0:T(8,128)(2,1)}) %all-gather.7.cloned.1.call-update) | async-done | bytes 3670032 | tf_op jit(solution)/shard_map/all_gather | solution.py:24
  91.9 0.0 copy-start.1
  91.9 2.6 %copy.6 = bf16[4,8,2,16,1792]{4,3,2,1,0:T(8,128)(2,1)S(1)} copy(bf16[4,8,2,16,1792]{4,3,0,1,2:T(8,128)(2,1)} %bitcast.15) | data formatting | bytes 7340032 | tf_op jit(solution)/shard_map/transpose | solution.py:27
  94.5 1.6 copy-done.1
  96.1 10.3 %fusion.2 = f32[1024,2020]{0,1:T(8,128)} fusion(bf16[1024,1792]{1,0:T(8,128)(2,1)S(1)} %bitcast.16, bf16[1792,2020]{0,1:T(8,128)(2,1)S(1)} %copy-done.1), kind=kOutput, calls=%fused_computation.10 | convolution fusion | flops 7413432320 | bytes 19183616 | tf_op jit(solution)/shard_map/dot_general | solution.py:64
  106.4 0.0 reduce-scatter.2.cloned.1.call-update
  106.4 83.2 %reduce-scatter.2.cloned.1.call-done = f32[256,2020]{0,1:T(8,128)} async-done(((f32[1024,2020]{0,1:T(8,128)}), f32[256,2020]{0,1:T(8,128)}) %reduce-scatter.2.cloned.1.call-update) | async-done | bytes 2068496 | tf_op jit(solution)/shard_map/reduce_scatter | solution.py:63
  189.6 0.0 copy-start
  189.6 2.0 reduce_max.18
  191.6 20.2 %all_to_all.18 = f32[64,1,256]{2,1,0:T(1,128)S(1)} all-to-all(f32[64,1,256]{2,1,0:T(1,128)S(1)} %broadcast_in_dim.4), channel_id=1, replica_groups=mesh['vocab_0'=4,'vocab_1'=8,'vocab_2'=2,'hidden'=4] {'vocab_0','vocab_1..., dimensions={0} | all-to-all | bytes 131072 | tf_op jit(solution)/shard_map/all_to_all | solution.py:37
  211.8 0.1 reduce_max.19
  211.9 0.0 copy-done
  211.9 1.6 exponential_reduce_fusion
  213.6 13.6 %all_to_all.19 = f32[64,1,256]{2,1,0:T(1,128)S(1)} all-to-all(f32[64,1,256]{2,1,0:T(1,128)S(1)} %broadcast_in_dim.5), channel_id=1, replica_groups=mesh['vocab_0'=4,'vocab_1'=8,'vocab_2'=2,'hidden'=4] {'vocab_0','vocab_1..., dimensions={0} | all-to-all | bytes 131072 | tf_op jit(solution)/shard_map/all_to_all | solution.py:37
  227.3 0.1 reduce_sum.19
  227.4 2.9 %subtract_maximum_fusion = f32[256,2020]{0,1:T(8,128)} fusion(f32[256]{0:T(256)S(1)} %log.7, f32[256,2020]{0,1:T(8,128)S(1)} %copy-done, f32[256]{0:T(256)S(1)} %reduce_max.19), kind=kLoop, calls=%fused_computation.3 | loop fusion | flops 7239680 | bytes 4139008 | tf_op jit(solution)/shard_map/max | solution.py:72
  (4 shorter events, 0.1 us)
Async XLA Ops:
  6.5 62.3 %all-gather.5.cloned.1.call-start = ((), (), s32[]{:S(2)}) async-start(), calls=%async_computation.5 | async-start | bytes 2064384 | tf_op jit(solution)/shard_map/all_gather | solution.py:24
  27.1 64.9 %all-gather.7.cloned.1.call-start = ((), (), s32[]{:S(2)}) async-start(), calls=%async_computation.6 | async-start | bytes 5505024 | tf_op jit(solution)/shard_map/all_gather | solution.py:24
  68.9 120.7 %reduce-scatter.2.cloned.1.call-start = ((), (), s32[]{:S(2)}) async-start(), calls=%async_computation.4 | async-start | bytes 10362880 | tf_op jit(solution)/shard_map/reduce_scatter | solution.py:63
  91.9 4.2 %copy-start.1 = (bf16[1792,2020]{0,1:T(8,128)(2,1)S(1)}, bf16[1792,2020]{0,1:T(8,128)(2,1)}, u32[]{:S(2)}) copy-start(bf16[1792,2020]{0,1:T(8,128)(2,1)} %param.3) | copy-start | bytes 21719044
  189.6 22.4 %copy-start = (f32[256,2020]{0,1:T(8,128)S(1)}, f32[256,2020]{0,1:T(8,128)}, u32[]{:S(2)}) copy-start(f32[256,2020]{0,1:T(8,128)} %reduce-scatter.2.cloned.1.call-done) | copy-start | bytes 6205444
Sparse Core Ops, SparseCore 0:
  27.2 41.6 all-gather.4
  70.6 21.2 all-gather.6
  106.5 83.0 reduce-scatter.1
